TPU v7x, 256 devices: a whole 4x4x8 slice. The times are simulated.
256 devices in a mesh: pair: 32 (over y, x, core), tm: 8 (over z).
Axes of the slice: x: 4, y: 4, z: 8, core: 2. Of those that a mesh axis runs over, the one named last changes fastest.
Arguments:
- three_centre: bfloat16 [1536, 65536], P(None, 'pair'), may hold values from -0.046875 to 0.046875
- root_coulomb: bfloat16 [1536, 1536], P(('pair', 'tm')), may hold values from -0.15625 to 0.15625
- occ_depth: float32 [256], replicated, may hold values from 0.1 to 1
- vir_energy: float32 [1024], replicated, may hold values from 0.01 to 500
- occ_block: int32 [256], P('pair'), may hold values from 0 to 15
- vir_block: int32 [256], P('pair'), may hold values from 0 to 63
Outputs:
- screened: float32 [8, 1536, 1536], P('tm', 'pair')
All inputs are finite; a program needn't handle non-finite values.
Results may differ from a plain program's by a relative error of at most 0.003.
Values may be sent and summed in bfloat16 or wider, within the bound.
A program may use at most 128 MiB of HBM per device.

v0:
```python
import math
import jax
import jax.numpy as jnp
from jax import lax
from jax.sharding import PartitionSpec as P

OB = 16
VB = 16
NOB = 16
NVB = 64
TIME_DEV = 1
log_span = math.log(5000.0)


def shards(three_centre, root_coulomb, occ_depth, vir_energy, occ_block, vir_block):
    n_pair = lax.axis_size("pair")
    n_times = lax.axis_size("tm") * TIME_DEV
    naux = three_centre.shape[0]
    rows = naux // n_pair
    occ_table = occ_depth.reshape(NOB, OB)
    vir_table = vir_energy.reshape(NVB, VB)
    occ_onehot = (occ_block[:, None] == jnp.arange(NOB, dtype=jnp.int32)[None, :]).astype(
        jnp.float32
    )
    vir_onehot = (vir_block[:, None] == jnp.arange(NVB, dtype=jnp.int32)[None, :]).astype(
        jnp.float32
    )
    occ_sel = jnp.dot(occ_onehot, occ_table, precision=lax.Precision.HIGHEST)
    vir_sel = jnp.dot(vir_onehot, vir_table, precision=lax.Precision.HIGHEST)
    gap = (occ_sel[:, :, None] + vir_sel[:, None, :]).reshape(-1)
    steps_t = jnp.arange(n_times).astype(jnp.float32)
    taus = 0.002 * jnp.exp(steps_t * (log_span / max(n_times - 1, 1)))
    omegas = (steps_t + 0.5) / n_times
    coef = 2.4 * omegas[:, None] * jnp.cos(jnp.pi * omegas[:, None] * (steps_t[None, :] + 0.5))
    first_freq = lax.axis_index("tm") * TIME_DEV
    my_coef = lax.dynamic_slice_in_dim(coef, first_freq, TIME_DEV, 0)
    decays = jnp.exp(-gap[None, :] * taus[:, None])
    weights = jnp.dot(my_coef, decays, precision=lax.Precision.HIGHEST)
    weighted = (three_centre.astype(jnp.float32) * weights[0][None, :]).astype(jnp.bfloat16)
    blocks = lax.dot_general(
        weighted, three_centre, (((1,), (1,)), ((), ())), preferred_element_type=jnp.float32
    )
    chi_flat = lax.psum_scatter(blocks, "pair", scatter_dimension=0, tiled=True)
    chi_low = chi_flat.reshape(rows, TIME_DEV, naux).transpose(1, 0, 2).astype(jnp.bfloat16)
    return jnp.einsum(
        "frc,cd->frd",
        chi_low,
        lax.all_gather(root_coulomb, ("pair", "tm"), axis=0, tiled=True),
        preferred_element_type=jnp.float32,
    )


def solution(mesh):
    in_specs = (P(None, "pair"), P(("pair", "tm"), None), P(), P(), P("pair"), P("pair"))
    out_specs = P("tm", "pair", None)
    return jax.shard_map(shards, mesh=mesh, in_specs=in_specs, out_specs=out_specs, check_vma=False)
```

profile of v0, /device:TPU:5, one launch (start us, length us, event | category | flops | bytes accessed | tf_op | source)
XLA Modules:
  0.0 154.7 jit_solution(11968216570324839412)
XLA Ops:
  7.4 0.0 all-gather.3.cloned.1.call-start
  7.4 0.7 all-gather.3.cloned.1.call-update
  8.1 0.0 reduce-scatter.2.cloned.1.call-start
  8.1 0.8 reshape.59
  8.9 0.8 reshape.58
  9.7 0.8 fusion.8
  10.5 0.8 fusion.9
  11.3 0.1 add_negate_fusion
  11.4 0.1 neg.12
  11.6 0.1 cosine_multiply_fusion
  11.7 0.3 fusion.3
  11.9 16.1 %fusion = f32[1536,1536]{1,0:T(8,128)} fusion(bf16[1536,2048]{1,0:T(8,128)(2,1)} %param.6, f32[2048]{0:T(1024)S(1)} %bitcast.13), kind=kOutput, calls=%fused_computation.1 | convolution fusion | flops 9673113600 | bytes 15736832 | tf_op jit(solution)/shard_map/dot_general | solution.py:40
  28.1 0.0 reduce-scatter.2.cloned.1.call-update
  28.1 106.7 %all-gather.3.cloned.1.call-done = bf16[256,6,1536]{2,1,0:T(8,128)(2,1)} async-done(((bf16[1,6,1536]{2,1,0:T(8,128)(2,1)}), bf16[256,6,1536]{2,1,0:T(8,128)(2,1)}) %all-gather.3.cloned.1.call-update) | async-done | bytes 4718608 | tf_op jit(solution)/shard_map/all_gather | solution.py:48
  134.8 8.4 %reshape.61 = bf16[1536,1536]{1,0:T(8,128)(2,1)} reshape(bf16[256,6,1536]{2,1,0:T(8,128)(2,1)} %all-gather.3.cloned.1.call-done) | data formatting | bytes 9437184
  143.2 0.0 reduce-scatter.2.cloned.1.call-done
  143.2 4.1 %convolution_bitcast_fusion = f32[1,48,1536]{2,1,0:T(8,128)} fusion(bf16[1536,1536]{1,0:T(8,128)(2,1)} %reshape.61, f32[48,1536]{1,0:T(8,128)} %reduce-scatter.2.cloned.1.call-done), kind=kOutput, calls=%fused_computation.3 | convolution fusion | flops 226566144 | bytes 5308416 | tf_op jit(solution)/shard_map/frc,cd->frd/dot_general | solution.py:45
  (3 shorter events, 0.0 us)
Async XLA Ops:
  7.4 127.4 %all-gather.3.cloned.1.call-start = ((), (), s32[]{:S(2)}) async-start(), calls=%async_computation.2 | async-start | bytes 6316032 | tf_op jit(solution)/shard_map/all_gather | solution.py:48
  8.1 135.1 %reduce-scatter.2.cloned.1.call-start = ((), (), s32[]{:S(2)}) async-start(), calls=%async_computation.1 | async-start | bytes 9732096 | tf_op jit(solution)/shard_map/reduce_scatter | solution.py:43
Sparse Core Ops, SparseCore 0:
  12.0 122.7 all-gather.2
Sparse Core Ops, SparseCore 1:
  28.2 106.9 reduce-scatter.1
where the time goes:
time: 155 us
  waiting for transfers between devices  107 us (69%)
  matrix products  22.1 us (14%)
  between operations  14.9 us (10%)
  local copies, waits for them, and re-layouts  10 us (6%)
    all_gather x1, waiting for transfers between devices, shards(): lax.all_gather(root_coulomb, ('pair', 'tm'), axis=0, tiled=True)  107 us
    dot_general x1, matrix products, shards(): lax.dot_general(weighted, three_centre, (((1,), (1,)), ((), ())), preferr...  16.1 us
    unnamed x1, local copies, waits for them, and re-layouts  8.4 us
    dot_general x1, matrix products, shards(): jnp.einsum('frc,cd->frd', chi_low, lax.all_gather(root_coulomb, ('pair',...  4.06 us
  transfers between devices with their start and end apart: 2, of which 1 were waited for; matrix products, arithmetic and copies ran while one was open for 18% of the time, Pallas kernels for 0%

commit v1 on v0

--- a/solution.py
+++ b/solution.py
@@ -45,7 +45,12 @@
     return jnp.einsum(
         "frc,cd->frd",
         chi_low,
-        lax.all_gather(root_coulomb, ("pair", "tm"), axis=0, tiled=True),
+        jnp.concatenate(
+            lax.all_to_all(
+                jnp.stack([root_coulomb] * lax.axis_size(("pair", "tm"))), ("pair", "tm"), 0, 0
+            ),
+            axis=0,
+        ),
         preferred_element_type=jnp.float32,
     )
 

time: 155 us -> 206 us (1.33)
  blocking collectives: 0 us -> 157 us
  waiting for transfers between devices: 107 us -> 0.02 us
    all_to_all x0 -> x1, blocking collectives: none -> 157 us  [shards(): lax.all_to_all(jnp.stack([root_coulomb] * lax.axis_size(('pair', 'tm'))),...]
    all_gather x1 -> x0, waiting for transfers between devices: 107 us -> none  [shards(): lax.all_gather(root_coulomb, ('pair', 'tm'), axis=0, tiled=True)]
    reshape x0 -> x1, local copies, waits for them, and re-layouts: none -> 8.42 us  [shards(): jnp.concatenate(lax.all_to_all(jnp.stack([root_coulomb] * lax.axis_size((...]
    unnamed x1 -> x2, local copies, waits for them, and re-layouts: 8.4 us -> 0.71 us
  transfers between devices with their start and end apart: 2 -> 1, of which waited for: 1 -> 0; matrix products, arithmetic and copies ran while one was open for 18% -> 4% of each run, Pallas kernels for 0% -> 0%
where the time goes in v1:
time: 206 us; the launch traced here: 204 us
  blocking collectives  157 us (76%)
  matrix products  22.2 us (11%)
  between operations  13.4 us (7%)
  local copies, waits for them, and re-layouts  11.1 us (5%)
    all_to_all x1, blocking collectives, shards(): lax.all_to_all(jnp.stack([root_coulomb] * lax.axis_size(('pair', 'tm'))),...  157 us
    dot_general x1, matrix products, shards(): lax.dot_general(weighted, three_centre, (((1,), (1,)), ((), ())), preferr...  16.1 us
    reshape x1, local copies, waits for them, and re-layouts, shards(): jnp.concatenate(lax.all_to_all(jnp.stack([root_coulomb] * lax.axis_size((...  8.42 us
  transfers between devices with their start and end apart: 1, of which 0 were waited for; matrix products, arithmetic and copies ran while one was open for 4% of the time, Pallas kernels for 0%

profile of v1, /device:TPU:5, one launch (start us, length us, event | category | flops | bytes accessed | tf_op | source)
XLA Modules:
  0.0 204.4 jit_solution(13249209204213022646)
XLA Ops:
  6.5 0.0 reduce-scatter.2.cloned.1.call-start
  6.6 0.8 reshape.64
  7.3 0.8 reshape.63
  8.1 0.8 fusion.9
  8.9 0.9 fusion.8
  9.8 0.1 add_negate_fusion
  9.9 0.1 neg.12
  10.0 0.1 cosine_multiply_fusion
  10.1 0.3 fusion.3
  10.3 16.1 %fusion = f32[1536,1536]{1,0:T(8,128)} fusion(bf16[1536,2048]{1,0:T(8,128)(2,1)} %param.6, f32[2048]{0:T(1024)S(1)} %bitcast.11), kind=kOutput, calls=%fused_computation.1 | convolution fusion | flops 9673113600 | bytes 15736832 | tf_op jit(solution)/shard_map/dot_general | solution.py:40
  26.5 0.0 copy-start
  26.5 0.0 reduce-scatter.2.cloned.1.call-update
  26.5 0.7 copy-done
  27.2 0.4 stack.2
  27.6 157.4 %all_to_all.5 = bf16[256,6,1536]{2,1,0:T(8,128)(2,1)} all-to-all(bf16[256,6,1536]{2,1,0:T(8,128)(2,1)S(1)} %stack.2), channel_id=1, replica_groups=mesh['pair'=32,'tm'=8] {'pair','tm'}, dimensions={0} | all-to-all | bytes 9437184 | tf_op jit(solution)/shard_map/all_to_all | solution.py:49
  185.1 8.4 %reshape.65 = bf16[1536,1536]{1,0:T(8,128)(2,1)} reshape(bf16[256,6,1536]{2,1,0:T(8,128)(2,1)} %all_to_all.5) | data formatting | bytes 9437184 | tf_op jit(solution)/shard_map/reshape | solution.py:48
  193.5 0.0 reduce-scatter.2.cloned.1.call-done
  193.5 4.1 %convolution_bitcast_fusion = f32[1,48,1536]{2,1,0:T(8,128)} fusion(bf16[1536,1536]{1,0:T(8,128)(2,1)} %reshape.65, f32[48,1536]{1,0:T(8,128)} %reduce-scatter.2.cloned.1.call-done), kind=kOutput, calls=%fused_computation.3 | convolution fusion | flops 226566144 | bytes 5308416 | tf_op jit(solution)/shard_map/frc,cd->frd/dot_general | solution.py:45
  (3 shorter events, 0.0 us)
Async XLA Ops:
  6.5 186.9 %reduce-scatter.2.cloned.1.call-start = ((), (), s32[]{:S(2)}) async-start(), calls=%async_computation.2 | async-start | bytes 9732096 | tf_op jit(solution)/shard_map/reduce_scatter | solution.py:43
  26.5 0.7 copy-start
Sparse Core Ops, SparseCore 0:
  26.6 124.2 reduce-scatter.1
